TPU v7x, 32 devices: a whole 2x2x4 slice. The times are simulated.
32 devices in a mesh: cube: 2 (over core), row: 4 (over y, x), col: 4 (over z).
Axes of the slice: x: 2, y: 2, z: 4, core: 2. Of those that a mesh axis runs over, the one named last changes fastest.
Arguments:
- child_update: float32 [2, 8192, 8192], P('cube', 'row', 'col'), may hold values from -8 to 80, as said below
- child_panel: bfloat16 [2, 8192, 2048], P('cube', 'row'), may hold values from -8 to 8
- parent_front: bfloat16 [16384, 16384], P('row', ('cube', 'col')), may hold values from -8 to 520, as said below
- block_map: int32 [2, 64], replicated, may hold values from 0 to 127, as said below
Outputs:
- schur: float32 [16384, 16384], P('row', ('cube', 'col'))
- panel: float32 [16384, 512], P('row')
Inputs may be any that keep to these rules, and one draw needn't show every extreme that they name: child_update[k] is symmetric for every child. parent_front is symmetric, and the leading 512 x 512 block of front is positive definite. `block_map`: for each child the 64 entries are distinct. Split a child's entries into aligned groups of 16 entries. In every group, for each r from 0 to 3, exactly 4 entries e have e // 32 equal to r. In every group, at most 2 entries share one value of e // 16, and every group has a value shared by 2 entries.
All inputs are finite; a program needn't handle non-finite values.
Results may differ from a plain program's by a relative error of at most 0.00044.
Values may be sent and summed in bfloat16 or wider, within the bound.
A program may use at most 320 MiB of HBM per device.

v0:
```python
import jax
import jax.numpy as jnp
from jax import lax
from jax.sharding import PartitionSpec as P

BLK = 128
PANEL = 512


def broadcast(block, axis, holder):
    block = jnp.where(lax.axis_index(axis) == holder, block, jnp.zeros_like(block))
    return lax.psum(block, axis)


def group_ranks(labels):
    count_all = labels.shape[-1]
    position = jnp.arange(count_all)
    before = position[:, None] > position[None, :]
    same_label = labels[..., :, None] == labels[..., None, :]
    return jnp.sum(jnp.logical_and(same_label, before), axis=-1)


def slot_tables(block_map, grid_rows, grid_cols, row_cap, col_cap, range_rows, range_cols):
    children = block_map.shape[0]
    grouped = block_map.reshape(children, grid_rows, -1)
    group_blocks = grouped.shape[2]
    row_dest = grouped // range_rows
    col_dest = grouped // range_cols
    row_slot = row_dest * row_cap + group_ranks(row_dest)
    col_slot = col_dest * col_cap + group_ranks(col_dest)
    members = jnp.arange(group_blocks, dtype=jnp.int32)
    row_hits = (row_slot[..., :, None] == members).astype(jnp.int32)
    send_rows = jnp.sum(row_hits * members[:, None], axis=2)
    row_local = jnp.sum(row_hits * (grouped % range_rows)[..., None], axis=2)
    col_slots = jnp.arange(grid_cols * col_cap, dtype=jnp.int32)
    col_hits = (col_slot[..., :, None] == col_slots).astype(jnp.int32)
    filled = jnp.sum(col_hits, axis=2) > 0
    send_cols = jnp.where(filled, jnp.sum(col_hits * members[:, None], axis=2), group_blocks)
    col_local = jnp.where(filled, jnp.sum(col_hits * (grouped % range_cols)[..., None], axis=2), -1)
    return (send_rows, row_local, send_cols, col_local)


def solve_rows(factor, raw_rows):
    result_rows = jax.scipy.linalg.solve_triangular(factor, raw_rows.T, lower=True).T
    return result_rows


def body(child_update, child_panel, parent_front, block_map):
    grid_rows = lax.axis_size("row")
    cube_count = lax.axis_size("cube")
    col_count = lax.axis_size("col")
    grid_cols = cube_count * col_count
    child_index = lax.axis_index("cube")
    row_index = lax.axis_index("row")
    col_index = lax.axis_index("col")
    range_index = lax.axis_index(("cube", "col"))
    group_blocks = child_update.shape[1] // BLK
    row_cap = group_blocks // grid_rows
    col_cap = max(1, group_blocks // grid_cols)
    front_rows, front_cols = parent_front.shape
    range_rows = front_rows // BLK
    range_cols = front_cols // BLK
    tiles_total = range_rows * range_cols
    own_panel = child_panel[0]
    column_panel = broadcast(own_panel, "row", col_index)
    contribution = child_update[0] - lax.dot_general(
        own_panel, column_panel, (((1,), (1,)), ((), ())), preferred_element_type=jnp.float32
    )
    send_rows, row_local, send_cols, col_local = slot_tables(
        block_map, grid_rows, grid_cols, row_cap, col_cap, range_rows, range_cols
    )
    my_rows = send_rows[child_index, row_index]
    my_cols = send_cols[child_index, col_index]
    blocks = contribution.reshape(group_blocks, BLK, group_blocks, BLK)
    by_row = jnp.take(blocks, my_rows, axis=0)
    incoming_rows = lax.dynamic_slice_in_dim(row_local, row_index * row_cap, row_cap, 2)
    incoming_cols = lax.dynamic_slice_in_dim(col_local, range_index * col_cap, col_cap, 2)
    packed = jnp.take(by_row, my_cols, axis=2, mode="fill", fill_value=0.0)
    packed = packed.reshape(grid_rows, row_cap, BLK, cube_count, col_count, col_cap, BLK)
    packed = packed.transpose(3, 0, 4, 1, 2, 5, 6).reshape(
        cube_count * grid_rows * col_count, row_cap * BLK, col_cap * BLK
    )
    arrived = lax.all_to_all(
        packed, ("cube", "row", "col"), split_axis=0, concat_axis=0, tiled=True
    )
    arrived = arrived.reshape(
        cube_count, grid_rows, col_count, row_cap, BLK, col_cap, BLK
    ).transpose(0, 1, 2, 3, 5, 4, 6)
    target_rows = incoming_rows[:, :, None, :, None]
    target_cols = incoming_cols[:, None, :, None, :]
    targets = jnp.where(target_cols >= 0, target_rows * range_cols + target_cols, tiles_total)
    pieces = arrived.reshape(-1, BLK, BLK)
    summed = jax.ops.segment_sum(pieces, targets.reshape(-1), num_segments=tiles_total)
    assembled = (
        summed.reshape(range_rows, range_cols, BLK, BLK)
        .transpose(0, 2, 1, 3)
        .reshape(front_rows, front_cols)
    )
    front_tile = parent_front.astype(jnp.float32) + assembled
    pivot_block = broadcast(front_tile[:PANEL, :PANEL], "row", 0)
    local_factor = jnp.linalg.cholesky(pivot_block)
    global_rows = row_index * front_rows + jnp.arange(front_rows)
    pivot_rows = global_rows[:, None] < PANEL

    def finish_rows(factor, solved):
        padded_pivot = jnp.concatenate(
            [factor, jnp.zeros((front_rows - PANEL, PANEL), jnp.float32)], axis=0
        )
        return jnp.where(pivot_rows, padded_pivot, solved)

    owner_rows = lax.cond(
        range_index == 0,
        lambda: finish_rows(local_factor, solve_rows(local_factor, front_tile[:, :PANEL])),
        lambda: jnp.zeros((front_rows, PANEL), jnp.float32),
    )
    panel_rows = broadcast(owner_rows, ("cube", "col"), 0)
    panel_low = panel_rows.astype(jnp.bfloat16)
    first_col = range_index * front_cols
    crossed = broadcast(panel_low, "row", first_col // front_rows)
    column_low = lax.dynamic_slice_in_dim(crossed, first_col % front_rows, front_cols, 0)
    update = front_tile - lax.dot_general(
        panel_low, column_low, (((1,), (1,)), ((), ())), preferred_element_type=jnp.float32
    )
    global_cols = first_col + jnp.arange(front_cols)
    keep_mask = (global_rows[:, None] >= PANEL) & (global_cols[None, :] >= PANEL)
    schur_tile = jnp.where(keep_mask, update, jnp.zeros_like(update))
    return (schur_tile, panel_rows)


def solution(mesh):
    placed = (P("cube", "row", "col"), P("cube", "row", None), P("row", ("cube", "col")), P())
    return jax.shard_map(
        body,
        mesh=mesh,
        in_specs=placed,
        out_specs=(P("row", ("cube", "col")), P("row", None)),
        check_vma=False,
    )
```

profile of v0, /device:TPU:0, one launch (start us, length us, event | category | flops | bytes accessed | tf_op | source)
XLA Modules:
  0.0 1507.9 jit_solution(11700483400209119964)
XLA Ops:
  7.2 7.3 bitcast_select_fusion
  15.3 17.8 %copy.60 = f32[1,2048,2048]{1,2,0:T(8,128)} copy(f32[1,2048,2048]{2,1,0:T(8,128)} %param.6) | data formatting | bytes 33554432 | tf_op args[0]
  35.2 154.3 %all-reduce.7.cloned.1.call-done = bf16[2048,2048]{1,0:T(8,128)(2,1)} async-done(((bf16[2048,2048]{1,0:T(8,128)(2,1)}), bf16[2048,2048]{1,0:T(8,128)(2,1)}) %all-reduce.7.cloned.1.call-update) | async-done | bytes 8388624 | tf_op jit(solution)/shard_map/psum | solution.py:12
  189.5 26.3 %fusion.24 = f32[256,8,16,128]{3,1,2,0:T(8,128)} fusion(f32[1,2048,2048]{1,2,0:T(8,128)} %copy.60, bf16[2048,2048]{1,0:T(8,128)(2,1)} %all-reduce.7.cloned.1.call-done, bf16[1,2048,2048]{2,1,0:T(8,128)(2,1)} %param.7), kind=kOutput, calls=%fused_computation.51 | convolution fusion | flops 17184063488 | bytes 50331648 | tf_op jit(solution)/shard_map/dot_general | solution.py:66
  215.8 14.2 copy.81
  229.9 21.5 %copy.61 = f32[16,128,16,128]{3,2,1,0:T(8,128)} copy(f32[16,128,16,128]{1,0,3,2:T(8,128)} %bitcast.101) | data formatting | bytes 33554432 | tf_op jit(solution)/shard_map/reshape | solution.py:74
  251.4 14.3 gather_fusion
  265.7 6.9 broadcast_select_fusion
  272.6 8.0 copy.62
  280.6 14.0 gather_fusion.1
  294.6 29.3 %fusion.25 = f32[2,4,4,4,128,2,128]{6,5,4,3,2,1,0:T(2,128)} fusion(f32[4,4,128,2,4,2,128]{6,2,1,0,5,4,3:T(8,128)} %bitcast.99, pred[2,4,2]{2,1,0:T(4,128)(4,1)S(1)} %compare_and_fusion), kind=kLoop, calls=%fused_computation.53 | loop fusion | flops 4194304 | bytes 33554448 | tf_op jit(solution)/shard_map/transpose | solution.py:80
  323.9 21.6 %reshape.390 = f32[32,512,256]{2,1,0:T(8,128)} reshape(f32[2,4,4,4,128,2,128]{6,5,4,3,2,1,0:T(2,128)} %fusion.25) | data formatting | bytes 33554432 | tf_op jit(solution)/shard_map/reshape | solution.py:80
  345.5 5.4 all-to-all-start
  351.3 20.9 %copy.59 = bf16[4096,2048]{0,1:T(8,128)(2,1)} copy(bf16[4096,2048]{1,0:T(8,128)(2,1)} %param.8) | data formatting | bytes 33554432 | tf_op args[2]
  372.3 336.7 %all-to-all-done = f32[32,512,256]{2,1,0:T(8,128)} async-done(((f32[32,512,256]{2,1,0:T(8,128)}), f32[32,512,256]{2,1,0:T(8,128)}, u32[]{:S(2)}, u32[]{:S(2)}) %all-to-all-start) | async-done | bytes 16777248 | tf_op jit(solution)/shard_map/all_to_all | solution.py:83
  709.0 20.8 %reshape.391 = f32[2,4,4,4,128,2,128]{6,5,4,3,2,1,0:T(2,128)} reshape(f32[32,512,256]{2,1,0:T(8,128)} %all-to-all-done) | data formatting | bytes 33554432 | tf_op jit(solution)/shard_map/reshape | solution.py:86
  729.7 12.7 copy.64
  742.4 11.5 broadcast_in_dim.87
  753.9 51.6 %scatter_fusion = f32[512,128,128]{2,1,0:T(8,128)} fusion(f32[512,128,128]{2,1,0:T(8,128)} %broadcast_in_dim.87, s32[256]{0:T(256)S(1)} %reshape.432, f32[256,128,128]{2,1,0:T(8,128)} %bitcast.100), kind=kCustom, calls=%fused_computation.2 | custom fusion | flops 4194304 | bytes 50332672 | tf_op jit(solution)/shard_map/scatter-add | solution.py:93
  805.4 34.6 %copy.65 = f32[32,128,16,128]{1,0,3,2:T(8,128)} copy(f32[32,128,16,128]{3,1,2,0:T(8,128)} %bitcast.97) | data formatting | bytes 67108864 | tf_op jit(solution)/shard_map/transpose | solution.py:96
  840.0 37.0 %bitcast_add_fusion = f32[4096,2048]{0,1:T(8,128)S(1)} fusion(f32[256,8,32,128]{3,2,1,0:T(8,128)} %bitcast.98, bf16[4096,2048]{0,1:T(8,128)(2,1)} %copy.59), kind=kLoop, calls=%fused_computation.48 | loop fusion | flops 16777216 | bytes 83886080 | tf_op jit(solution)/shard_map/add | solution.py:99
  877.0 11.7 copy-done
  888.7 1.1 slice_select_fusion
  890.2 65.8 %all-reduce.9.cloned.1.call-done = f32[512,512]{0,1:T(8,128)} async-done(((f32[512,512]{0,1:T(8,128)}), f32[512,512]{0,1:T(8,128)}) %all-reduce.9.cloned.1.call-update) | async-done | bytes 1048592 | tf_op jit(solution)/shard_map/psum | solution.py:12
  956.0 1.6 copy.66
  957.6 1.4 fusion.29
  959.1 11.7 cholesky.103
  970.9 9.8 custom-call.33
  981.4 11.7 cholesky.212
  993.1 9.9 custom-call.34
  1003.7 11.7 cholesky.228
  1015.5 9.8 custom-call.35
  1025.9 12.3 cholesky.240
  1038.5 1.2 broadcast_in_dim.95
  1039.7 100.5 %conditional.1 = (f32[4096,512]{1,0:T(8,128)}) conditional(s32[]{:T(128)} %convert_element_type.23, () %tuple.39, (s32[]{:T(128)}, s32[4096,1]{0,1:T(1,128)S(1)}, s32[512,512]{0,1:T(8,128)S(1)}, s32[512,512]{0,1:T(8,128)S(1)}, s32[128,128]{1,0:T(8,128)S(1)}, /*index=5*/s32[128,128]{1,0:T(8,128)S(1)}, s32[128,128]{1,0:T(8,128)S(1)}, ...), branch_computations={%region_10.11_spmd, %region_11.20_spmd} | conditional | flops 8068735488 | bytes 104493288 | solution.py:111
  1039.9 0.7 compare_reduce_fusion.3
  1042.2 0.9 copy.71
  1044.5 1.3 copy.73
  1046.0 0.9 copy.72
  1047.6 0.7 compare_reduce_fusion.1
  1049.0 3.0 fusion.15
  1052.1 12.2 while.1
  1052.8 2.2 dynamic-slice.7
  1055.8 2.2 dynamic-slice.7
  1058.9 2.3 dynamic-slice.7
  1061.9 2.2 dynamic-slice.7
  1064.2 39.6 %custom-call.29 = f32[4,128,128]{1,2,0:T(8,128)S(1)} custom-call(f32[4,128,128]{2,1,0:T(8,128)S(1)} %get-tuple-element.210), custom_call_target="InvertDiagBlocksLowerTriangular" | custom-call | tf_op jit(solution)/shard_map/cond/branch_1_fun/jit(_solve_triangular)/triangular_solve | solution.py:44
  1103.8 3.9 slice_bitcast_fusion
  1107.8 1.9 fusion.13
  1109.7 2.8 convolution_subtract_fusion.1
  1112.5 1.9 fusion.21
  1114.4 3.3 convolution_subtract_fusion
  1117.8 1.9 fusion.19
  1119.7 5.5 fusion.7
  1125.2 1.9 fusion.18
  1127.2 3.9 fusion
  1131.1 8.9 copy.79
  1140.2 7.8 broadcast_select_fusion.1
  1148.1 172.8 %all-reduce.11.cloned.1.call-done = f32[4096,512]{1,0:T(8,128)} async-done(((f32[4096,512]{1,0:T(8,128)}), f32[4096,512]{1,0:T(8,128)}) %all-reduce.11.cloned.1.call-update) | async-done | bytes 8388624 | tf_op jit(solution)/shard_map/psum | solution.py:12
  1321.0 5.8 broadcast_select_fusion.2
  1326.8 103.8 %all-reduce.13.cloned.1.call-done = bf16[4096,512]{1,0:T(8,128)(2,1)} async-done(((bf16[4096,512]{1,0:T(8,128)(2,1)}), bf16[4096,512]{1,0:T(8,128)(2,1)}) %all-reduce.13.cloned.1.call-update) | async-done | bytes 4194320 | tf_op jit(solution)/shard_map/psum | solution.py:12
  1430.7 29.4 %subtract_select_fusion = f32[4096,2048]{0,1:T(8,128)} fusion(f32[4096,2048]{0,1:T(8,128)} %copy-done, pred[4096]{0:T(1024)(128)(4,1)S(1)} %add_compare_fusion, pred[2048]{0:T(1024)(128)(4,1)S(1)} %add_compare_fusion.1, bf16[4096,512]{1,0:T(8,128)(2,1)} %all-reduce.13.cloned.1.call-done, s32[]{:T(128)S(6)} %select_n.218, ...), kind=kOutput, calls=%fused_computation.49 | convolution fusion | flops 8617197568 | bytes 77600768 | tf_op jit(solution)/shard_map/dot_general | solution.py:121
  1460.1 33.3 %copy.76 = f32[4096,2048]{1,0:T(8,128)} copy(f32[4096,2048]{0,1:T(8,128)} %subtract_select_fusion) | data formatting | bytes 67108864
  1493.4 7.8 copy.111
  (83 shorter events, 11.1 us)
Async XLA Ops:
  7.2 182.3 %all-reduce.7.cloned.1.call-start = ((), (), s32[]{:S(2)}) async-start(), calls=%async_computation.1 | async-start | bytes 16777216 | tf_op jit(solution)/shard_map/psum | solution.py:12
  14.5 0.7 copy-start.2
  345.5 363.5 %all-to-all-start = ((f32[32,512,256]{2,1,0:T(8,128)}), f32[32,512,256]{2,1,0:T(8,128)}, u32[]{:S(2)}, u32[]{:S(2)}) async-start(f32[32,512,256]{2,1,0:T(8,128)} %reshape.390), calls=%async_computation | async-start | bytes 33554432 | tf_op jit(solution)/shard_map/all_to_all | solution.py:83
  350.9 605.1 %all-reduce.9.cloned.1.call-start = ((), (), s32[]{:S(2)}) async-start(), calls=%async_computation.2 | async-start | bytes 2097152 | tf_op jit(solution)/shard_map/psum | solution.py:12
  877.0 11.7 copy-start
  889.8 431.2 %all-reduce.11.cloned.1.call-start = ((), (), s32[]{:S(2)}) async-start(), calls=%async_computation.3 | async-start | bytes 16777216 | tf_op jit(solution)/shard_map/psum | solution.py:12
  1015.4 22.8 %copy-start.1 = (f32[128,128]{1,0:T(8,128)}, f32[128,128]{1,0:T(8,128)S(1)}, u32[]{:S(2)}) copy-start(f32[128,128]{1,0:T(8,128)S(1)} %cholesky.228) | copy-start | bytes 196612
  1148.0 282.6 %all-reduce.13.cloned.1.call-start = ((), (), s32[]{:S(2)}) async-start(), calls=%async_computation.4 | async-start | bytes 8388608 | tf_op jit(solution)/shard_map/psum | solution.py:12
Sparse Core Ops, SparseCore 0:
  14.7 174.7 all-reduce.6
  889.9 66.0 all-reduce.8
  1148.2 172.7 all-reduce.10
  1326.9 103.7 all-reduce.12
where the time goes:
time: 1520 us; the launch traced here: 1510 us
  waiting for transfers between devices  833 us (55%)
  local copies, waits for them, and re-layouts  298 us (20%)
  other arithmetic  276 us (18%)
  matrix products  77 us (5%)
    psum x4, waiting for transfers between devices, broadcast(): return lax.psum(block, axis)  497 us
    all_to_all x1, waiting for transfers between devices, body(): lax.all_to_all(packed, ('cube', 'row', 'col'), split_axis=0, concat_axis=...  337 us
    unnamed x11, local copies, waits for them, and re-layouts  106 us
    another operation x16, other arithmetic, body(): local_factor = jnp.linalg.cholesky(pivot_block)  79.9 us
    scatter-add x1, other arithmetic, body(): jax.ops.segment_sum(pieces, targets.reshape(-1), num_segments=tiles_total)  51.6 us
    another operation x3, other arithmetic, solve_rows(): jax.scipy.linalg.solve_triangular(factor, raw_rows.T, lower=True)  42.6 us
    add x1, other arithmetic, body(): front_tile = parent_front.astype(jnp.float32) + assembled  37 us
    transpose x1, local copies, waits for them, and re-layouts, body(): assembled = summed.reshape(range_rows, range_cols, BLK, BLK).transpose(0,...  34.6 us
  transfers between devices with their start and end apart: 5, of which 5 were waited for; matrix products, arithmetic and copies ran while one was open for 3% of the time, Pallas kernels for 0%

commit v1 on v0

--- a/solution.py
+++ b/solution.py
@@ -9,7 +9,7 @@
 
 def broadcast(block, axis, holder):
     block = jnp.where(lax.axis_index(axis) == holder, block, jnp.zeros_like(block))
-    return lax.psum(block, axis)
+    return jnp.sum(lax.all_gather(block, axis), axis=0)
 
 
 def group_ranks(labels):

time: 1520 us -> 2200 us (1.45)
  waiting for transfers between devices: 833 us -> 1410 us
  other arithmetic: 276 us -> 331 us
  local copies, waits for them, and re-layouts: 298 us -> 350 us
    all_gather x0 -> x4, waiting for transfers between devices: none -> 1050 us  [broadcast(): return jnp.sum(lax.all_gather(block, axis), axis=0)]
    psum x4 -> x0, waiting for transfers between devices: 497 us -> none  [broadcast(): return lax.psum(block, axis)]
    reduce_sum x0 -> x4, other arithmetic: none -> 69.5 us  [broadcast(): return jnp.sum(lax.all_gather(block, axis), axis=0)]
    another operation x27 -> x29, local copies, waits for them, and re-layouts: 15.6 us -> 48.5 us
    all_gather x0 -> x1, local copies, waits for them, and re-layouts: none -> 27.8 us  [broadcast(): return jnp.sum(lax.all_gather(block, axis), axis=0)]
    unnamed x11 -> x8, local copies, waits for them, and re-layouts: 106 us -> 111 us
  transfers between devices with their start and end apart: 5 -> 5, of which waited for: 5 -> 5; matrix products, arithmetic and copies ran while one was open for 3% -> 1% of each run, Pallas kernels for 0% -> 0%
where the time goes in v1:
time: 2200 us; the launch traced here: 2190 us
  waiting for transfers between devices  1410 us (64%)
  local copies, waits for them, and re-layouts  350 us (16%)
  other arithmetic  331 us (15%)
  matrix products  78.1 us (4%)
    all_gather x4, waiting for transfers between devices, broadcast(): return jnp.sum(lax.all_gather(block, axis), axis=0)  1050 us
    all_to_all x1, waiting for transfers between devices, body(): lax.all_to_all(packed, ('cube', 'row', 'col'), split_axis=0, concat_axis=...  358 us
    unnamed x8, local copies, waits for them, and re-layouts  111 us
    another operation x16, other arithmetic, body(): local_factor = jnp.linalg.cholesky(pivot_block)  80.3 us
    reduce_sum x4, other arithmetic, broadcast(): return jnp.sum(lax.all_gather(block, axis), axis=0)  69.5 us
    scatter-add x1, other arithmetic, body(): jax.ops.segment_sum(pieces, targets.reshape(-1), num_segments=tiles_total)  51.6 us
    another operation x29, local copies, waits for them, and re-layouts  48.5 us
  transfers between devices with their start and end apart: 5, of which 5 were waited for; matrix products, arithmetic and copies ran while one was open for 1% of the time, Pallas kernels for 0%

profile of v1, /device:TPU:0, one launch (start us, length us, event | category | flops | bytes accessed | tf_op | source)
XLA Modules:
  0.0 2191.7 jit_solution(15719169210905084738)
XLA Ops:
  7.2 7.3 broadcast_select_fusion.1
  15.3 18.7 copy.85
  36.2 278.4 %all-gather.8.cloned.1.call-done = bf16[4,2048,2048]{2,1,0:T(8,128)(2,1)} async-done(((bf16[1,2048,2048]{2,1,0:T(8,128)(2,1)}), bf16[4,2048,2048]{2,1,0:T(8,128)(2,1)}) %all-gather.8.cloned.1.call-update) | async-done | bytes 33554448 | tf_op jit(solution)/shard_map/all_gather | solution.py:12
  314.5 16.6 reduce_sum.112
  331.1 26.3 %fusion.24 = f32[256,8,16,128]{3,1,2,0:T(8,128)} fusion(f32[1,2048,2048]{1,2,0:T(8,128)} %copy.85, bf16[2048,2048]{1,0:T(8,128)(2,1)} %reduce_sum.112, bf16[1,2048,2048]{2,1,0:T(8,128)(2,1)} %param.7), kind=kOutput, calls=%fused_computation.52 | convolution fusion | flops 17184063488 | bytes 50331648 | tf_op jit(solution)/shard_map/dot_general | solution.py:66
  357.4 14.2 copy.103
  371.5 21.5 copy.86
  393.0 14.5 gather_fusion
  407.5 6.9 broadcast_select_fusion
  414.4 8.0 copy.87
  422.4 13.8 gather_fusion.1
  436.2 29.3 %fusion.25 = f32[2,4,4,4,128,2,128]{6,5,4,3,2,1,0:T(2,128)} fusion(f32[4,4,128,2,4,2,128]{6,2,1,0,5,4,3:T(8,128)} %bitcast.104, pred[2,4,2]{2,1,0:T(4,128)(4,1)S(1)} %compare_and_fusion), kind=kLoop, calls=%fused_computation.54 | loop fusion | flops 4194304 | bytes 33554448 | tf_op jit(solution)/shard_map/transpose | solution.py:80
  465.5 21.6 reshape.404
  487.1 4.7 all-to-all-start
  492.3 357.6 %all-to-all-done = f32[32,512,256]{2,1,0:T(8,128)} async-done(((f32[32,512,256]{2,1,0:T(8,128)}), f32[32,512,256]{2,1,0:T(8,128)}, u32[]{:S(2)}, u32[]{:S(2)}) %all-to-all-start) | async-done | bytes 16777248 | tf_op jit(solution)/shard_map/all_to_all | solution.py:83
  849.9 21.2 reshape.405
  871.1 12.7 copy.89
  883.7 11.5 broadcast_in_dim.87
  895.2 51.6 %scatter_fusion = f32[512,128,128]{2,1,0:T(8,128)} fusion(f32[512,128,128]{2,1,0:T(8,128)} %broadcast_in_dim.87, s32[256]{0:T(256)S(1)} %reshape.446, f32[256,128,128]{2,1,0:T(8,128)} %bitcast.105), kind=kCustom, calls=%fused_computation.2 | custom fusion | flops 4194304 | bytes 50332672 | tf_op jit(solution)/shard_map/scatter-add | solution.py:93
  946.8 31.7 %copy.90 = f32[32,128,16,128]{3,2,1,0:T(8,128)} copy(f32[32,128,16,128]{3,1,2,0:T(8,128)} %bitcast.102) | data formatting | bytes 67108864 | tf_op jit(solution)/shard_map/transpose | solution.py:96
  978.5 23.0 %bitcast_add_fusion = f32[4096,2048]{1,0:T(8,128)S(1)} fusion(f32[512,8,16,128]{3,2,1,0:T(8,128)} %bitcast.103, bf16[4096,2048]{1,0:T(8,128)(2,1)} %param.8), kind=kLoop, calls=%fused_computation.49 | loop fusion | flops 16777216 | bytes 83886080 | tf_op jit(solution)/shard_map/add | solution.py:99
  1001.6 11.7 copy-done
  1013.3 1.1 slice_select_fusion
  1014.6 66.1 %all-gather.10.cloned.1.call-done = f32[2048,512]{1,0:T(8,128)} async-done(((f32[512,512]{1,0:T(8,128)}), f32[2048,512]{1,0:T(8,128)}) %all-gather.10.cloned.1.call-update) | async-done | bytes 4194320 | tf_op jit(solution)/shard_map/all_gather | solution.py:12
  1080.7 2.8 reduce_sum.113
  1084.1 11.7 cholesky.103
  1095.9 9.8 custom-call.33
  1106.4 11.7 cholesky.212
  1118.1 10.0 custom-call.34
  1128.8 11.7 cholesky.228
  1140.5 9.8 custom-call.35
  1151.0 12.7 cholesky.240
  1163.9 1.1 broadcast_in_dim.95
  1165.0 123.9 %conditional.1 = (f32[4096,512]{0,1:T(8,128)}) conditional(s32[]{:T(128)} %convert_element_type.35, () %tuple.39, (s32[]{:T(128)}, s32[4096,1]{0,1:T(1,128)S(1)}, s32[512,512]{0,1:T(8,128)S(1)}, s32[512,512]{0,1:T(8,128)S(1)}, s32[128,128]{1,0:T(8,128)S(1)}, /*index=5*/s32[128,128]{1,0:T(8,128)S(1)}, s32[128,128]{1,0:T(8,128)S(1)}, ...), branch_computations={%region_10.11_spmd, %region_11.20_spmd} | conditional | flops 8068735488 | bytes 156922080 | solution.py:111
  1168.8 1.3 copy.98
  1170.4 0.9 copy.97
  1173.3 2.5 copy.99
  1175.8 3.0 fusion.15
  1178.8 12.2 while.1
  1179.5 2.2 dynamic-slice.7
  1182.6 2.3 dynamic-slice.7
  1185.6 2.2 dynamic-slice.7
  1188.7 2.2 dynamic-slice.7
  1191.0 39.3 %custom-call.29 = f32[4,128,128]{1,2,0:T(8,128)S(1)} custom-call(f32[4,128,128]{2,1,0:T(8,128)S(1)} %get-tuple-element.210), custom_call_target="InvertDiagBlocksLowerTriangular" | custom-call | tf_op jit(solution)/shard_map/cond/branch_1_fun/jit(_solve_triangular)/triangular_solve | solution.py:44
  1230.3 31.3 %copy.100 = f32[4096,2048]{0,1:T(8,128)} copy(f32[4096,2048]{1,0:T(8,128)} %get-tuple-element.358) | data formatting | bytes 67108864 | tf_op jit(solution)/shard_map
  1261.6 3.9 slice_bitcast_fusion
  1265.5 1.9 fusion.13
  1267.4 2.8 convolution_subtract_fusion.1
  1270.2 1.9 fusion.21
  1272.2 3.3 convolution_subtract_fusion
  1275.5 1.9 fusion.19
  1277.5 5.3 fusion.7
  1282.7 1.9 fusion.18
  1284.7 4.0 fusion
  1288.9 7.8 broadcast_select_fusion.2
  1296.9 561.3 %all-gather.12.cloned.1.call-done = f32[32768,512]{0,1:T(8,128)} async-done(((f32[4096,512]{0,1:T(8,128)}), f32[32768,512]{0,1:T(8,128)}) %all-gather.12.cloned.1.call-update) | async-done | bytes 67108880 | tf_op jit(solution)/shard_map/all_gather | solution.py:12
  1858.2 56.3 %copy.105 = f32[64,8,8,4096]{3,2,1,0:T(8,128)} copy(f32[64,8,8,4096]{3,1,2,0:T(8,128)} %bitcast.43) | data formatting | bytes 134217728
  1914.5 25.1 %bitcast_reduce_fusion = f32[4096,512]{0,1:T(8,128)} fusion(f32[64,8,8,4096]{3,2,1,0:T(8,128)} %copy.105), kind=kLoop, calls=%fused_computation.48 | loop fusion | flops 14680064 | bytes 75497472 | tf_op jit(solution)/shard_map/reduce_sum | solution.py:12
  1939.6 5.7 broadcast_select_fusion.3
  1945.4 9.5 copy.101
  1954.9 146.1 %all-gather.14.cloned.1.call-done = bf16[16384,512]{0,1:T(8,128)(2,1)} async-done(((bf16[4096,512]{0,1:T(8,128)(2,1)}), bf16[16384,512]{0,1:T(8,128)(2,1)}) %all-gather.14.cloned.1.call-update) | async-done | bytes 16777232 | tf_op jit(solution)/shard_map/all_gather | solution.py:12
  2101.0 27.8 %reshape.454 = bf16[4,4096,512]{1,0,2:T(4,128)(2,1)} reshape(bf16[16384,512]{0,1:T(8,128)(2,1)} %all-gather.14.cloned.1.call-done) | data formatting | bytes 33554432 | tf_op jit(solution)/shard_map/all_gather | solution.py:12
  2128.8 25.0 %reduce_sum.115 = bf16[4096,512]{0,1:T(8,128)(2,1)} reduce(bf16[4,4096,512]{1,0,2:T(4,128)(2,1)} %reshape.454, bf16[]{:T(256)} %constant.292.clone.1), dimensions={0}, to_apply=%region_21.22 | reduce | flops 6291456 | bytes 20971522 | tf_op jit(solution)/shard_map/reduce_sum | solution.py:12
  2153.8 30.9 %subtract_select_fusion = f32[4096,2048]{1,0:T(8,128)} fusion(f32[4096,2048]{1,0:T(8,128)} %copy-done, pred[2048]{0:T(1024)(128)(4,1)S(1)} %add_compare_fusion.1, pred[4096]{0:T(1024)(128)(4,1)S(1)} %add_compare_fusion, bf16[4096,512]{0,1:T(8,128)(2,1)} %reduce_sum.115, s32[]{:T(128)S(6)} %select_n.230, f32[4096,512]{0,1:T(8,128)} %bitcast_reduce_fusion), kind=kOutput, calls=%fused_computation.50 | convolution fusion | flops 8617197568 | bytes 77600768 | tf_op jit(solution)/shard_map/dot_general | solution.py:121
  (86 shorter events, 12.9 us)
Async XLA Ops:
  7.2 307.4 %all-gather.8.cloned.1.call-start = ((), (), s32[]{:S(2)}) async-start(), calls=%async_computation.1 | async-start | bytes 41943040 | tf_op jit(solution)/shard_map/all_gather | solution.py:12
  14.5 0.7 copy-start.1
  487.1 362.8 %all-to-all-start = ((f32[32,512,256]{2,1,0:T(8,128)}), f32[32,512,256]{2,1,0:T(8,128)}, u32[]{:S(2)}, u32[]{:S(2)}) async-start(f32[32,512,256]{2,1,0:T(8,128)} %reshape.404), calls=%async_computation | async-start | bytes 33554432 | tf_op jit(solution)/shard_map/all_to_all | solution.py:83
  491.8 588.9 %all-gather.10.cloned.1.call-start = ((), (), s32[]{:S(2)}) async-start(), calls=%async_computation.2 | async-start | bytes 5242880 | tf_op jit(solution)/shard_map/all_gather | solution.py:12
  1001.6 11.7 copy-start
  1014.4 843.8 %all-gather.12.cloned.1.call-start = ((), (), s32[]{:S(2)}) async-start(), calls=%async_computation.3 | async-start | bytes 75497472 | tf_op jit(solution)/shard_map/all_gather | solution.py:12
  1296.8 804.2 %all-gather.14.cloned.1.call-start = ((), (), s32[]{:S(2)}) async-start(), calls=%async_computation.4 | async-start | bytes 20971520 | tf_op jit(solution)/shard_map/all_gather | solution.py:12
Sparse Core Ops, SparseCore 0:
  14.7 299.7 all-gather.7
  1014.5 66.1 all-gather.9
  1296.9 561.1 all-gather.11
  1945.5 155.4 all-gather.13
